TPU v7x, 256 devices: a whole 4x4x8 slice. The times are simulated.
256 devices in a mesh: emit: 8 (over y, z_hi), client: 32 (over x, z_lo, core).
Axes of the slice: x: 4, y: 4, z: 8 (z_hi: 2, z_lo: 4; z = z_hi * 4 + z_lo), core: 2. Of those that a mesh axis runs over, the one named last changes fastest.
Arguments:
- features: bfloat16 [131072, 768], P('client'), may hold values from -28 to 28
- labels: int32 [131072], P('client'), may hold values from 0 to 999
- client_ids: int32 [256], replicated, may hold values from 0 to 255, each once
- trunk_in: bfloat16 [256, 2048], replicated, may hold values from -6 to 6
- trunk_weight: bfloat16 [2048, 2048], P(None, 'client'), may hold values from -0.125 to 0.125
- class_table: bfloat16 [1000, 2048], P('emit'), may hold values from -6 to 6
- emit_weight: bfloat16 [2048, 768], P('emit'), may hold values from -0.125 to 0.125
Outputs:
- loss: float32 [131072], P('client')
- emit_grad: float32 [2048, 768], P(('emit', 'client'))
- trunk_grad: float32 [2048, 2048], P(None, ('emit', 'client'))
Inputs may be any that keep to these rules, and one draw needn't show every extreme that they name: Each client number appears once; slot s holds the features of client client_ids[s].
All inputs are finite; a program needn't handle non-finite values.
Results may differ from a plain program's by a relative error of at most 0.022.
Values may be sent and summed in bfloat16 or wider, within the bound.
A program may use at most 128 MiB of HBM per device.

v0:
```python
import jax
import jax.numpy as jnp
from jax import lax
from jax.sharding import PartitionSpec as P

CL_DEV = 8


def sent_to_all(x, axis):
    count = lax.axis_size(axis)
    return lax.all_to_all(jnp.broadcast_to(x[None], (count, *x.shape)), axis, 0, 0, tiled=True)


def laid_out(parts, dim):
    parts = jnp.moveaxis(parts, 0, dim)
    lengths = parts.shape
    return parts.reshape(*lengths[:dim], lengths[dim] * lengths[dim + 1], *lengths[dim + 2 :])


def gather_directly(x, axis, dim):
    parts = sent_to_all(x, axis)
    return laid_out(parts, dim)


def taken_together(x, axis):
    everything = sent_to_all(x, axis)
    return jnp.max(everything, axis=0)


def of_everyone(x, axis):
    return sent_to_all(x, axis).astype(jnp.float32).sum(axis=0)


def in_blocks(x, dim, count):
    lengths = x.shape
    parts = x.reshape(*lengths[:dim], count, lengths[dim] // count, *lengths[dim + 1 :])
    return jnp.moveaxis(parts, dim, 0)


def sum_at_owner(x, axis, dim):
    parts = in_blocks(x, dim, lax.axis_size(axis))
    arrived = lax.all_to_all(parts, axis, split_axis=0, concat_axis=0, tiled=True)
    return arrived.astype(jnp.float32).sum(axis=0)


def silu_grad(value):
    sig = jax.nn.sigmoid(value)
    return sig * (1.0 + value * (1.0 - sig))


def per_device(features, labels, client_ids, trunk_in, trunk_weight, class_table, emit_weight):
    slots = CL_DEV
    clients = trunk_in.shape[0]
    hidden_dim = trunk_in.shape[1]
    classes = class_table.shape[0]
    feat_dim = features.shape[1]
    samples = features.shape[0] // slots
    client_index = lax.axis_index("client")
    emit_index = lax.axis_index("emit")
    pre_cols = jnp.dot(trunk_in, trunk_weight, preferred_element_type=jnp.float32).astype(
        jnp.bfloat16
    )
    pre_all = gather_directly(pre_cols, "client", 1)
    own_ids = lax.dynamic_slice_in_dim(client_ids, client_index * slots, slots)
    numbers = lax.iota(jnp.int32, clients)
    picker = (own_ids[:, None] == numbers[None, :]).astype(jnp.bfloat16)
    pre_own = jnp.dot(picker, pre_all, preferred_element_type=jnp.float32)
    code_in = jax.nn.silu(pre_own)[:, None, :] + class_table.astype(jnp.float32)[None, :, :]
    code = jax.nn.silu(code_in).astype(jnp.bfloat16).reshape(slots * classes, hidden_dim)
    emit_full = lax.all_gather(emit_weight, "emit", axis=0, tiled=True)
    heads = jnp.dot(code, emit_full, preferred_element_type=jnp.float32).astype(jnp.bfloat16)
    heads = heads.reshape(slots, classes, feat_dim)
    feats = features.reshape(slots, samples, feat_dim)
    logits = jnp.einsum("snd,skd->snk", feats, heads, preferred_element_type=jnp.float32)
    class_ids = emit_index * classes + lax.iota(jnp.int32, classes)
    onehot = (labels.reshape(slots, samples)[:, :, None] == class_ids[None, None, :]).astype(
        jnp.float32
    )
    target = jnp.sum(logits * onehot, axis=2)
    local_top = jnp.max(logits, axis=2)
    top = taken_together(local_top, "emit")
    expd = jnp.exp(logits - top[:, :, None])
    total, target_all = (
        of_everyone(jnp.sum(expd, axis=2).astype(jnp.bfloat16), "emit").astype(jnp.float32),
        of_everyone(target.astype(jnp.bfloat16), "emit").astype(jnp.float32),
    )
    loss = (top + jnp.log(total) - target_all).reshape(slots * samples)
    grad_logits = ((expd / total[:, :, None] - onehot) / clients).astype(jnp.bfloat16)
    grad_heads = jnp.einsum("snk,snd->skd", grad_logits, feats, preferred_element_type=jnp.float32)
    grad_heads = grad_heads.astype(jnp.bfloat16).reshape(slots * classes, feat_dim)
    partial_rows = lax.psum_scatter(
        jnp.einsum("rh,rd->hd", code, grad_heads, preferred_element_type=jnp.float32).astype(
            jnp.bfloat16
        ),
        "emit",
        scatter_dimension=0,
        tiled=True,
    )
    emit_grad = sum_at_owner(partial_rows, "client", 0)
    grad_code = jnp.dot(grad_heads, emit_full.T, preferred_element_type=jnp.float32)
    grad_code = grad_code.reshape(slots, classes, hidden_dim)
    grad_sum = jnp.sum(grad_code * silu_grad(code_in), axis=1)
    block = hidden_dim // lax.axis_size("emit")
    grad_block = sum_at_owner(grad_sum.astype(jnp.bfloat16), "emit", 1)
    pre_block = lax.dynamic_slice_in_dim(pre_own, emit_index * block, block, 1)
    grad_pre = (grad_block * silu_grad(pre_block)).astype(jnp.bfloat16)
    grad_all = gather_directly(grad_pre, "client", 0)
    width = block // lax.axis_size("client")
    grad_mine = lax.dynamic_slice_in_dim(grad_all, client_index * width, width, 1)
    picker_all = (client_ids[:, None] == numbers[None, :]).astype(jnp.bfloat16)
    grad_client = jnp.einsum(
        "sc,sw->cw", picker_all, grad_mine, preferred_element_type=jnp.float32
    ).astype(jnp.bfloat16)
    trunk_grad = jnp.einsum("ch,cw->hw", trunk_in, grad_client, preferred_element_type=jnp.float32)
    return (loss, emit_grad, trunk_grad)


def solution(mesh):
    return jax.shard_map(
        per_device,
        mesh=mesh,
        in_specs=(
            P("client", None),
            P("client"),
            P(),
            P(),
            P(None, "client"),
            P("emit", None),
            P("emit", None),
        ),
        out_specs=(P("client"), P(("emit", "client"), None), P(None, ("emit", "client"))),
        check_vma=False,
    )
```

profile of v0, /device:TPU:1, one launch (start us, length us, event | category | flops | bytes accessed | tf_op | source)
XLA Modules:
  0.0 302.1 jit_solution(12591394443601378770)
XLA Ops:
  7.2 0.0 copy-start
  7.2 0.0 copy-start.5
  7.2 0.0 all-gather.2.cloned.1.call-start
  7.2 0.7 all-gather.2.cloned.1.call-update
  7.9 0.5 copy-done
  8.4 1.4 convolution_convert_fusion.1
  9.8 1.1 broadcast_in_dim.10
  10.9 10.0 %all-to-all-start = ((bf16[32,256,64]{1,2,0:T(8,128)(2,1)}), bf16[32,256,64]{1,2,0:T(8,128)(2,1)S(1)}, u32[]{:S(2)}, u32[]{:S(2)}) async-start(bf16[32,256,64]{1,2,0:T(8,128)(2,1)} %broadcast_in_dim.10), calls=%async_computation | async-start | bytes 2097152 | tf_op jit(solution)/shard_map/all_to_all | solution.py:11
  20.9 1.1 convert_element_type.69
  22.1 0.0 copy-start.1
  22.1 0.0 copy-done.5
  22.1 0.1 dynamic_slice.9
  22.2 35.0 %all-to-all-done = bf16[32,256,64]{1,2,0:T(8,128)(2,1)S(1)} async-done(((bf16[32,256,64]{1,2,0:T(8,128)(2,1)}), bf16[32,256,64]{1,2,0:T(8,128)(2,1)S(1)}, u32[]{:S(2)}, u32[]{:S(2)}) %all-to-all-start) | async-done | bytes 1048608 | tf_op jit(solution)/shard_map/all_to_all | solution.py:11
  57.2 0.4 divide_multiply_fusion
  57.6 4.3 %broadcast_add_fusion = f32[8,125,2048]{2,1,0:T(8,128)} fusion(f32[125,2048]{1,0:T(8,128)S(1)} %convert_element_type.69, f32[8,2048]{1,0:T(8,128)S(1)} %get-tuple-element.5), kind=kLoop, calls=%fused_computation.16 | loop fusion | flops 2048000 | bytes 9281536 | tf_op jit(solution)/shard_map/add | solution.py:68
  61.9 0.0 copy-done.1
  61.9 7.9 %add.67 = f32[1000,2048]{1,0:T(8,128)} reshape(f32[8,125,2048]{2,1,0:T(8,128)} %broadcast_add_fusion) | data formatting | bytes 16384000 | tf_op jit(solution)/shard_map/add | solution.py:68
  69.8 41.8 %all-gather.2.cloned.1.call-done = bf16[2048,768]{1,0:T(8,128)(2,1)} async-done(((bf16[256,768]{1,0:T(8,128)(2,1)}), bf16[2048,768]{1,0:T(8,128)(2,1)}) %all-gather.2.cloned.1.call-update) | async-done | bytes 3145744 | tf_op jit(solution)/shard_map/all_gather | solution.py:70
  111.6 8.6 %fusion.23 = bf16[1000,768]{1,0:T(8,128)(2,1)S(1)} fusion(bf16[2048,768]{1,0:T(8,128)(2,1)} %all-gather.2.cloned.1.call-done, f32[1000,2048]{1,0:T(8,128)} %add.67), kind=kOutput, calls=%fused_computation.32 | convolution fusion | flops 3156736000 | bytes 12873728 | tf_op jit(solution)/shard_map/dot_general | solution.py:71
  120.2 1.6 reshape.60
  121.8 0.0 copy-start.4
  121.8 5.4 %bitcast_reduce_fusion = (f32[8,512]{1,0:T(8,128)S(1)}, f32[8,125,512]{2,1,0:T(8,128)S(1)}) fusion(bf16[8,125,768]{2,1,0:T(8,128)(2,1)} %reshape.60, bf16[8,512,768]{2,1,0:T(8,128)(2,1)} %bitcast.40), kind=kOutput, calls=%fused_computation.28 | convolution fusion | flops 786939904 | bytes 9891840 | tf_op jit(solution)/shard_map/snd,skd->snk/dot_general | solution.py:74
  127.3 0.6 broadcast_in_dim.11
  127.9 3.4 %all-to-all-start.1 = ((f32[8,8,512]{2,1,0:T(8,128)}), f32[8,8,512]{2,1,0:T(8,128)S(1)}, u32[]{:S(2)}, u32[]{:S(2)}) async-start(f32[8,8,512]{2,1,0:T(8,128)} %broadcast_in_dim.11), calls=%async_computation.1 | async-start | bytes 262144 | tf_op jit(solution)/shard_map/all_to_all | solution.py:11
  131.3 0.0 reduce-scatter.2.cloned.1.call-start
  131.3 0.0 copy-done.4
  131.4 9.3 %all-to-all-done.1 = f32[8,8,512]{2,1,0:T(8,128)S(1)} async-done(((f32[8,8,512]{2,1,0:T(8,128)}), f32[8,8,512]{2,1,0:T(8,128)S(1)}, u32[]{:S(2)}, u32[]{:S(2)}) %all-to-all-start.1) | async-done | bytes 131104 | tf_op jit(solution)/shard_map/all_to_all | solution.py:11
  140.7 0.6 fusion.22
  141.3 11.5 %all_to_all.35 = bf16[8,8,512]{2,1,0:T(8,128)(2,1)S(1)} all-to-all(bf16[8,8,512]{2,1,0:T(8,128)(2,1)S(1)} %broadcast_in_dim.12), channel_id=1, replica_groups=mesh['emit'=8,'client'=32] {'emit'}, dimensions={0} | all-to-all | bytes 131072 | tf_op jit(solution)/shard_map/all_to_all | solution.py:11
  152.8 0.0 copy-start.2
  152.8 4.1 %convolution_convert_fusion = bf16[8,125,768]{2,1,0:T(8,128)(2,1)S(1)} fusion(bf16[8,512,768]{2,1,0:T(8,128)(2,1)} %bitcast.41, f32[8,125,512]{2,1,0:T(8,128)S(1)} %get-tuple-element.8, f32[8,512]{1,0:T(8,128)S(1)} %convert_reduce_fusion.2, s32[8,512]{1,0:T(8,128)S(1)} %eq.44, f32[8,512]{1,0:T(8,128)S(1)} %reduce_max.19, s32[125]{0:T(128)S(1)} %iota_add_fusion), kind=kOutput, calls=%fused_computation.31 | convolution fusion | flops 790784000 | bytes 9925108 | tf_op jit(solution)/shard_map/snk,snd->skd/dot_general | solution.py:89
  156.9 0.0 copy-start.6
  156.9 1.1 copy-done.6
  158.1 0.0 copy-done.2
  158.1 0.0 copy-start.3
  158.1 5.7 %bitcast_convert_fusion = bf16[2048,768]{1,0:T(8,128)(2,1)} fusion(bf16[8,125,768]{2,1,0:T(8,128)(2,1)S(1)} %convolution_convert_fusion, f32[125,2048]{1,0:T(8,128)S(1)} %copy-done.2, f32[8,2048]{1,0:T(8,128)S(1)} %get-tuple-element.5), kind=kOutput, calls=%fused_computation.12 | convolution fusion | flops 3159588864 | bytes 5771264 | tf_op jit(solution)/shard_map/rh,rd->hd/dot_general | solution.py:92
  163.8 0.0 reduce-scatter.2.cloned.1.call-update
  163.8 0.0 copy-done.3
  163.8 8.1 %fusion.7 = bf16[8,2048]{1,0:T(8,128)(2,1)} fusion(bf16[8,125,768]{2,1,0:T(8,128)(2,1)} %copy-done.6, f32[125,2048]{1,0:T(8,128)S(1)} %copy-done.3, f32[8,2048]{1,0:T(8,128)S(1)} %get-tuple-element.5, bf16[2048,768]{1,0:T(8,128)(2,1)} %all-gather.2.cloned.1.call-done), kind=kOutput, calls=%fused_computation.10 | convolution fusion | flops 3166191616 | bytes 5804032 | tf_op jit(solution)/shard_map/dot_general | solution.py:100
  172.0 3.3 %all-to-all-start.5 = ((bf16[8,8,256]{2,1,0:T(8,128)(2,1)}), bf16[8,8,256]{2,1,0:T(8,128)(2,1)S(1)}, u32[]{:S(2)}, u32[]{:S(2)}) async-start(bf16[8,8,256]{2,1,0:T(8,128)(2,1)} %bitcast.8), calls=%async_computation.6 | async-start | bytes 65536 | tf_op jit(solution)/shard_map/all_to_all | solution.py:42
  175.3 9.0 %all-to-all-done.5 = bf16[8,8,256]{2,1,0:T(8,128)(2,1)S(1)} async-done(((bf16[8,8,256]{2,1,0:T(8,128)(2,1)}), bf16[8,8,256]{2,1,0:T(8,128)(2,1)S(1)}, u32[]{:S(2)}, u32[]{:S(2)}) %all-to-all-start.5) | async-done | bytes 32800 | tf_op jit(solution)/shard_map/all_to_all | solution.py:42
  184.4 0.6 broadcast_in_dim.13
  185.0 3.4 %all-to-all-start.3 = ((bf16[8,8,512]{2,1,0:T(8,128)(2,1)}), bf16[8,8,512]{2,1,0:T(8,128)(2,1)S(1)}, u32[]{:S(2)}, u32[]{:S(2)}) async-start(bf16[8,8,512]{2,1,0:T(8,128)(2,1)} %broadcast_in_dim.13), calls=%async_computation.3 | async-start | bytes 131072 | tf_op jit(solution)/shard_map/all_to_all | solution.py:11
  188.4 9.4 %all-to-all-done.3 = bf16[8,8,512]{2,1,0:T(8,128)(2,1)S(1)} async-done(((bf16[8,8,512]{2,1,0:T(8,128)(2,1)}), bf16[8,8,512]{2,1,0:T(8,128)(2,1)S(1)}, u32[]{:S(2)}, u32[]{:S(2)}) %all-to-all-start.3) | async-done | bytes 65568 | tf_op jit(solution)/shard_map/all_to_all | solution.py:11
  197.8 25.7 %all_to_all.36 = bf16[32,8,256]{2,1,0:T(8,128)(2,1)S(1)} all-to-all(bf16[32,8,256]{2,1,0:T(8,128)(2,1)S(1)} %broadcast_in_dim.14), channel_id=1, replica_groups=mesh['emit'=8,'client'=32] {'client'}, dimensions={0} | all-to-all | bytes 262144 | tf_op jit(solution)/shard_map/all_to_all | solution.py:11
  223.5 50.2 %reduce-scatter.2.cloned.1.call-done = bf16[256,768]{1,0:T(8,128)(2,1)} async-done(((bf16[2048,768]{1,0:T(8,128)(2,1)}), bf16[256,768]{1,0:T(8,128)(2,1)}) %reduce-scatter.2.cloned.1.call-update) | async-done | bytes 393232 | tf_op jit(solution)/shard_map/reduce_scatter | solution.py:91
  273.7 6.8 %all-to-all-start.4 = ((bf16[32,8,768]{2,1,0:T(8,128)(2,1)}), bf16[32,8,768]{2,1,0:T(8,128)(2,1)S(1)}, u32[]{:S(2)}, u32[]{:S(2)}) async-start(bf16[32,8,768]{2,1,0:T(8,128)(2,1)} %bitcast.43), calls=%async_computation.5 | async-start | bytes 786432 | tf_op jit(solution)/shard_map/all_to_all | solution.py:42
  280.6 0.6 copy.15
  281.2 1.1 convolution_bitcast_fusion
  282.3 12.3 %all-to-all-done.4 = bf16[32,8,768]{2,1,0:T(8,128)(2,1)S(1)} async-done(((bf16[32,8,768]{2,1,0:T(8,128)(2,1)}), bf16[32,8,768]{2,1,0:T(8,128)(2,1)S(1)}, u32[]{:S(2)}, u32[]{:S(2)}) %all-to-all-start.4) | async-done | bytes 393248 | tf_op jit(solution)/shard_map/all_to_all | solution.py:42
  294.6 0.7 convert_reduce_fusion
  (10 shorter events, 0.1 us)
Async XLA Ops:
  7.2 1.2 copy-start
  7.2 14.9 %copy-start.5 = (s32[256]{0:T(256)S(1)}, s32[256]{0:T(256)}, u32[]{:S(2)}) copy-start(s32[256]{0:T(256)} %param.9) | copy-start | bytes 3076
  7.2 104.4 %all-gather.2.cloned.1.call-start = ((), (), s32[]{:S(2)}) async-start(), calls=%async_computation.8 | async-start | bytes 3538944 | tf_op jit(solution)/shard_map/all_gather | solution.py:70
  10.9 46.3 %all-to-all-start = ((bf16[32,256,64]{1,2,0:T(8,128)(2,1)}), bf16[32,256,64]{1,2,0:T(8,128)(2,1)S(1)}, u32[]{:S(2)}, u32[]{:S(2)}) async-start(bf16[32,256,64]{1,2,0:T(8,128)(2,1)} %broadcast_in_dim.10), calls=%async_computation | async-start | bytes 2097152 | tf_op jit(solution)/shard_map/all_to_all | solution.py:11
  22.1 39.8 %copy-start.1 = (f32[125,2048]{1,0:T(8,128)}, f32[125,2048]{1,0:T(8,128)S(1)}, u32[]{:S(2)}) copy-start(f32[125,2048]{1,0:T(8,128)S(1)} %convert_element_type.69) | copy-start | bytes 3072004
  121.8 9.5 %copy-start.4 = (s32[4096]{0:T(1024)S(1)}, s32[4096]{0:T(1024)}, u32[]{:S(2)}) copy-start(s32[4096]{0:T(1024)} %param.8) | copy-start | bytes 49156
  127.9 12.8 %all-to-all-start.1 = ((f32[8,8,512]{2,1,0:T(8,128)}), f32[8,8,512]{2,1,0:T(8,128)S(1)}, u32[]{:S(2)}, u32[]{:S(2)}) async-start(f32[8,8,512]{2,1,0:T(8,128)} %broadcast_in_dim.11), calls=%async_computation.1 | async-start | bytes 262144 | tf_op jit(solution)/shard_map/all_to_all | solution.py:11
  131.3 142.4 %reduce-scatter.2.cloned.1.call-start = ((), (), s32[]{:S(2)}) async-start(), calls=%async_computation.9 | async-start | bytes 3538944 | tf_op jit(solution)/shard_map/reduce_scatter | solution.py:91
  152.8 5.3 %copy-start.2 = (f32[125,2048]{1,0:T(8,128)S(1)}, f32[125,2048]{1,0:T(8,128)}, u32[]{:S(2)}) copy-start(f32[125,2048]{1,0:T(8,128)} %copy-done.1) | copy-start | bytes 3072004
  156.9 1.1 copy-start.6
  158.1 5.8 %copy-start.3 = (f32[125,2048]{1,0:T(8,128)S(1)}, f32[125,2048]{1,0:T(8,128)}, u32[]{:S(2)}) copy-start(f32[125,2048]{1,0:T(8,128)} %copy-done.1) | copy-start | bytes 3072004
  172.0 12.4 %all-to-all-start.5 = ((bf16[8,8,256]{2,1,0:T(8,128)(2,1)}), bf16[8,8,256]{2,1,0:T(8,128)(2,1)S(1)}, u32[]{:S(2)}, u32[]{:S(2)}) async-start(bf16[8,8,256]{2,1,0:T(8,128)(2,1)} %bitcast.8), calls=%async_computation.6 | async-start | bytes 65536 | tf_op jit(solution)/shard_map/all_to_all | solution.py:42
  185.0 12.8 %all-to-all-start.3 = ((bf16[8,8,512]{2,1,0:T(8,128)(2,1)}), bf16[8,8,512]{2,1,0:T(8,128)(2,1)S(1)}, u32[]{:S(2)}, u32[]{:S(2)}) async-start(bf16[8,8,512]{2,1,0:T(8,128)(2,1)} %broadcast_in_dim.13), calls=%async_computation.3 | async-start | bytes 131072 | tf_op jit(solution)/shard_map/all_to_all | solution.py:11
  273.7 20.9 %all-to-all-start.4 = ((bf16[32,8,768]{2,1,0:T(8,128)(2,1)}), bf16[32,8,768]{2,1,0:T(8,128)(2,1)S(1)}, u32[]{:S(2)}, u32[]{:S(2)}) async-start(bf16[32,8,768]{2,1,0:T(8,128)(2,1)} %bitcast.43), calls=%async_computation.5 | async-start | bytes 786432 | tf_op jit(solution)/shard_map/all_to_all | solution.py:42
Sparse Core Ops, SparseCore 0:
  10.6 100.9 all-gather.1
  164.0 109.7 reduce-scatter.1
where the time goes:
time: 303 us; the launch traced here: 302 us
  waiting for transfers between devices  168 us (55%)
  blocking collectives  37.2 us (12%)
  matrix products  34.9 us (12%)
  starting transfers between devices  27 us (9%)
  local copies, waits for them, and re-layouts  14.3 us (5%)
  between operations  14.3 us (5%)
  other arithmetic  6.74 us (2%)
    all_to_all x3, waiting for transfers between devices, sent_to_all(): lax.all_to_all(jnp.broadcast_to(x[None], (count, *x.shape)), axis, 0, 0,...  53.7 us
    reduce_scatter x1, waiting for transfers between devices, per_device(): lax.psum_scatter(jnp.einsum('rh,rd->hd', code, grad_heads, preferred_elem...  50.2 us
    all_gather x1, waiting for transfers between devices, per_device(): emit_full = lax.all_gather(emit_weight, 'emit', axis=0, tiled=True)  41.8 us
    all_to_all x2, blocking collectives, sent_to_all(): lax.all_to_all(jnp.broadcast_to(x[None], (count, *x.shape)), axis, 0, 0,...  37.2 us
    all_to_all x2, waiting for transfers between devices, sum_at_owner(): lax.all_to_all(parts, axis, split_axis=0, concat_axis=0, tiled=True)  21.3 us
    all_to_all x3, starting transfers between devices, sent_to_all(): lax.all_to_all(jnp.broadcast_to(x[None], (count, *x.shape)), axis, 0, 0,...  16.7 us
    all_to_all x2, starting transfers between devices, sum_at_owner(): lax.all_to_all(parts, axis, split_axis=0, concat_axis=0, tiled=True)  10.1 us
    dot_general x1, matrix products, per_device(): jnp.dot(code, emit_full, preferred_element_type=jnp.float32)  8.6 us
  transfers between devices with their start and end apart: 7, of which 7 were waited for; matrix products, arithmetic and copies ran while one was open for 9% of the time, Pallas kernels for 0%

commit v1 on v0

--- a/solution.py
+++ b/solution.py
@@ -67,7 +67,9 @@
     pre_own = jnp.dot(picker, pre_all, preferred_element_type=jnp.float32)
     code_in = jax.nn.silu(pre_own)[:, None, :] + class_table.astype(jnp.float32)[None, :, :]
     code = jax.nn.silu(code_in).astype(jnp.bfloat16).reshape(slots * classes, hidden_dim)
-    emit_full = lax.all_gather(emit_weight, "emit", axis=0, tiled=True)
+    emit_full = jnp.concatenate(
+        lax.all_to_all(jnp.stack([emit_weight] * lax.axis_size("emit")), "emit", 0, 0), axis=0
+    )
     heads = jnp.dot(code, emit_full, preferred_element_type=jnp.float32).astype(jnp.bfloat16)
     heads = heads.reshape(slots, classes, feat_dim)
     feats = features.reshape(slots, samples, feat_dim)

time: 303 us -> 322 us (1.063)
  blocking collectives: 37.2 us -> 71.9 us
  waiting for transfers between devices: 168 us -> 156 us
    all_to_all x0 -> x1, waiting for transfers between devices: none -> 62.8 us  [per_device(): lax.all_to_all(jnp.stack([emit_weight] * lax.axis_size('emit')), 'emit',...]
    all_gather x1 -> x0, waiting for transfers between devices: 41.8 us -> none  [per_device(): emit_full = lax.all_gather(emit_weight, 'emit', axis=0, tiled=True)]
    all_to_all x3 -> x2, waiting for transfers between devices: 53.7 us -> 18.6 us  [sent_to_all(): lax.all_to_all(jnp.broadcast_to(x[None], (count, *x.shape)), axis, 0, 0,...]
    all_to_all x2 -> x3, blocking collectives: 37.2 us -> 71.9 us  [sent_to_all(): lax.all_to_all(jnp.broadcast_to(x[None], (count, *x.shape)), axis, 0, 0,...]
    all_to_all x3 -> x2, starting transfers between devices: 16.7 us -> 7.65 us  [sent_to_all(): lax.all_to_all(jnp.broadcast_to(x[None], (count, *x.shape)), axis, 0, 0,...]
    all_to_all x0 -> x1, starting transfers between devices: none -> 8.25 us  [per_device(): lax.all_to_all(jnp.stack([emit_weight] * lax.axis_size('emit')), 'emit',...]
    add x1 -> x0, local copies, waits for them, and re-layouts: 7.94 us -> none  [per_device(): jax.nn.silu(pre_own)[:, None, :]]
    convert_element_type x0 -> x1, local copies, waits for them, and re-layouts: none -> 5.34 us  [per_device(): jax.nn.silu(code_in).astype(jnp.bfloat16)]
  transfers between devices with their start and end apart: 7 -> 6, of which waited for: 7 -> 6; matrix products, arithmetic and copies ran while one was open for 9% -> 7% of each run, Pallas kernels for 0% -> 0%
where the time goes in v1:
time: 322 us
  waiting for transfers between devices  156 us (48%)
  blocking collectives  71.9 us (22%)
  matrix products  32.8 us (10%)
  starting transfers between devices  26.1 us (8%)
  local copies, waits for them, and re-layouts  14.6 us (5%)
  between operations  14.2 us (4%)
  other arithmetic  6.03 us (2%)
    all_to_all x3, blocking collectives, sent_to_all(): lax.all_to_all(jnp.broadcast_to(x[None], (count, *x.shape)), axis, 0, 0,...  71.9 us
    all_to_all x1, waiting for transfers between devices, per_device(): lax.all_to_all(jnp.stack([emit_weight] * lax.axis_size('emit')), 'emit',...  62.8 us
    reduce_scatter x1, waiting for transfers between devices, per_device(): lax.psum_scatter(jnp.einsum('rh,rd->hd', code, grad_heads, preferred_elem...  51.7 us
    all_to_all x2, waiting for transfers between devices, sum_at_owner(): lax.all_to_all(parts, axis, split_axis=0, concat_axis=0, tiled=True)  22.7 us
    all_to_all x2, waiting for transfers between devices, sent_to_all(): lax.all_to_all(jnp.broadcast_to(x[None], (count, *x.shape)), axis, 0, 0,...  18.6 us
    all_to_all x2, starting transfers between devices, sum_at_owner(): lax.all_to_all(parts, axis, split_axis=0, concat_axis=0, tiled=True)  10.2 us
    all_to_all x1, starting transfers between devices, per_device(): lax.all_to_all(jnp.stack([emit_weight] * lax.axis_size('emit')), 'emit',...  8.25 us
    dot_general x1, matrix products, per_device(): jnp.dot(grad_heads, emit_full.T, preferred_element_type=jnp.float32)  8.17 us
  transfers between devices with their start and end apart: 6, of which 6 were waited for; matrix products, arithmetic and copies ran while one was open for 7% of the time, Pallas kernels for 0%

profile of v1, /device:TPU:1, one launch (start us, length us, event | category | flops | bytes accessed | tf_op | source)
XLA Modules:
  0.0 321.5 jit_solution(13239166599386115456)
XLA Ops:
  7.2 0.0 copy-start
  7.2 0.0 copy-start.4
  7.2 1.2 copy-done
  8.4 1.4 convolution_convert_fusion.2
  9.8 0.1 broadcast_in_dim.10
  9.9 37.7 %all_to_all.40 = bf16[32,256,64]{1,2,0:T(8,128)(2,1)S(1)} all-to-all(bf16[32,256,64]{1,2,0:T(8,128)(2,1)S(1)} %broadcast_in_dim.10), channel_id=1, replica_groups=mesh['emit'=8,'client'=32] {'client'}, dimensions={0} | all-to-all | bytes 2097152 | tf_op jit(solution)/shard_map/all_to_all | solution.py:11
  47.6 0.0 copy-done.4
  47.6 1.9 stack.2
  49.5 0.0 copy-start.6
  49.5 8.3 %all-to-all-start.1 = ((bf16[8,256,768]{2,1,0:T(8,128)(2,1)}), bf16[8,256,768]{2,1,0:T(8,128)(2,1)}, u32[]{:S(2)}, u32[]{:S(2)}) async-start(bf16[8,256,768]{2,1,0:T(8,128)(2,1)} %stack.2), calls=%async_computation.1 | async-start | bytes 6291456 | tf_op jit(solution)/shard_map/all_to_all | solution.py:71
  57.8 1.1 convert_element_type.76
  58.9 0.0 copy-start.1
  58.9 0.0 copy-done.6
  59.0 0.1 dynamic_slice.9
  59.0 0.4 divide_multiply_fusion
  59.4 3.6 %fusion.3 = bf16[8,125,2048]{2,1,0:T(8,128)(2,1)} fusion(f32[125,2048]{1,0:T(8,128)S(1)} %convert_element_type.76, f32[8,2048]{1,0:T(8,128)S(1)} %get-tuple-element.5), kind=kLoop, calls=%fused_computation.6 | loop fusion | flops 12288000 | bytes 5185536 | tf_op jit(solution)/shard_map/convert_element_type | solution.py:69
  63.0 0.0 copy-done.1
  63.0 5.3 %convert_element_type.78 = bf16[1000,2048]{1,0:T(8,128)(2,1)} reshape(bf16[8,125,2048]{2,1,0:T(8,128)(2,1)} %fusion.3) | data formatting | bytes 8192000 | tf_op jit(solution)/shard_map/convert_element_type | solution.py:69
  68.3 62.8 %all-to-all-done.1 = bf16[8,256,768]{2,1,0:T(8,128)(2,1)} async-done(((bf16[8,256,768]{2,1,0:T(8,128)(2,1)}), bf16[8,256,768]{2,1,0:T(8,128)(2,1)}, u32[]{:S(2)}, u32[]{:S(2)}) %all-to-all-start.1) | async-done | bytes 3145760 | tf_op jit(solution)/shard_map/all_to_all | solution.py:71
  131.2 6.5 %convolution_convert_fusion.1 = bf16[1000,768]{1,0:T(8,128)(2,1)S(1)} fusion(bf16[1000,2048]{1,0:T(8,128)(2,1)} %convert_element_type.78, bf16[2048,768]{1,0:T(8,128)(2,1)} %bitcast.2), kind=kOutput, calls=%fused_computation.24 | convolution fusion | flops 3146496000 | bytes 8777728 | tf_op jit(solution)/shard_map/dot_general | solution.py:73
  137.7 1.6 reshape.75
  139.3 0.0 copy-start.5
  139.3 5.4 %bitcast_reduce_fusion = (f32[8,512]{1,0:T(8,128)S(1)}, f32[8,125,512]{2,1,0:T(8,128)S(1)}) fusion(bf16[8,125,768]{2,1,0:T(8,128)(2,1)} %reshape.75, bf16[8,512,768]{2,1,0:T(8,128)(2,1)} %bitcast.42), kind=kOutput, calls=%fused_computation.20 | convolution fusion | flops 786939904 | bytes 9891840 | tf_op jit(solution)/shard_map/snd,skd->snk/dot_general | solution.py:76
  144.7 0.7 broadcast_in_dim.11
  145.3 4.3 %all-to-all-start.2 = ((f32[8,8,512]{2,1,0:T(8,128)}), f32[8,8,512]{2,1,0:T(8,128)S(1)}, u32[]{:S(2)}, u32[]{:S(2)}) async-start(f32[8,8,512]{2,1,0:T(8,128)} %broadcast_in_dim.11), calls=%async_computation.2 | async-start | bytes 262144 | tf_op jit(solution)/shard_map/all_to_all | solution.py:11
  149.6 0.0 reduce-scatter.2.cloned.1.call-start
  149.7 0.0 copy-done.5
  149.7 9.4 %all-to-all-done.2 = f32[8,8,512]{2,1,0:T(8,128)S(1)} async-done(((f32[8,8,512]{2,1,0:T(8,128)}), f32[8,8,512]{2,1,0:T(8,128)S(1)}, u32[]{:S(2)}, u32[]{:S(2)}) %all-to-all-start.2) | async-done | bytes 131104 | tf_op jit(solution)/shard_map/all_to_all | solution.py:11
  159.1 0.6 fusion.13
  159.7 11.5 %all_to_all.41 = bf16[8,8,512]{2,1,0:T(8,128)(2,1)S(1)} all-to-all(bf16[8,8,512]{2,1,0:T(8,128)(2,1)S(1)} %broadcast_in_dim.12), channel_id=1, replica_groups=mesh['emit'=8,'client'=32] {'emit'}, dimensions={0} | all-to-all | bytes 131072 | tf_op jit(solution)/shard_map/all_to_all | solution.py:11
  171.3 0.0 copy-start.2
  171.3 4.1 %convolution_convert_fusion = bf16[8,125,768]{2,1,0:T(8,128)(2,1)S(1)} fusion(bf16[8,512,768]{2,1,0:T(8,128)(2,1)} %bitcast.43, f32[8,125,512]{2,1,0:T(8,128)S(1)} %get-tuple-element.8, f32[8,512]{1,0:T(8,128)S(1)} %convert_reduce_fusion.2, s32[8,512]{1,0:T(8,128)S(1)} %eq.44, f32[8,512]{1,0:T(8,128)S(1)} %reduce_max.19, s32[125]{0:T(128)S(1)} %iota_add_fusion), kind=kOutput, calls=%fused_computation.23 | convolution fusion | flops 790784000 | bytes 9925108 | tf_op jit(solution)/shard_map/snk,snd->skd/dot_general | solution.py:91
  175.4 0.0 copy-start.7
  175.4 1.1 copy-done.7
  176.5 0.0 copy-done.2
  176.5 5.7 %bitcast_convert_fusion = bf16[2048,768]{1,0:T(8,128)(2,1)} fusion(bf16[8,125,768]{2,1,0:T(8,128)(2,1)S(1)} %convolution_convert_fusion, f32[125,2048]{1,0:T(8,128)S(1)} %copy-done.2, f32[8,2048]{1,0:T(8,128)S(1)} %get-tuple-element.5), kind=kOutput, calls=%fused_computation.11 | convolution fusion | flops 3159588864 | bytes 5771264 | tf_op jit(solution)/shard_map/rh,rd->hd/dot_general | solution.py:94
  182.3 0.0 copy-start.3
  182.3 0.0 reduce-scatter.2.cloned.1.call-update
  182.3 1.2 copy-done.3
  183.5 8.2 %fusion.7 = bf16[8,2048]{1,0:T(8,128)(2,1)} fusion(bf16[8,125,768]{2,1,0:T(8,128)(2,1)} %copy-done.7, bf16[2048,768,1]{1,0,2:T(8,128)(2,1)} %bitcast.7, f32[125,2048]{1,0:T(8,128)S(1)} %copy-done.3, f32[8,2048]{1,0:T(8,128)S(1)} %get-tuple-element.5), kind=kOutput, calls=%fused_computation.10 | convolution fusion | flops 3166191616 | bytes 5804032 | tf_op jit(solution)/shard_map/dot_general | solution.py:102
  191.6 3.3 %all-to-all-start.6 = ((bf16[8,8,256]{2,1,0:T(8,128)(2,1)}), bf16[8,8,256]{2,1,0:T(8,128)(2,1)S(1)}, u32[]{:S(2)}, u32[]{:S(2)}) async-start(bf16[8,8,256]{2,1,0:T(8,128)(2,1)} %bitcast.9), calls=%async_computation.7 | async-start | bytes 65536 | tf_op jit(solution)/shard_map/all_to_all | solution.py:42
  195.0 10.4 %all-to-all-done.6 = bf16[8,8,256]{2,1,0:T(8,128)(2,1)S(1)} async-done(((bf16[8,8,256]{2,1,0:T(8,128)(2,1)}), bf16[8,8,256]{2,1,0:T(8,128)(2,1)S(1)}, u32[]{:S(2)}, u32[]{:S(2)}) %all-to-all-start.6) | async-done | bytes 32800 | tf_op jit(solution)/shard_map/all_to_all | solution.py:42
  205.4 0.6 broadcast_in_dim.13
  206.1 3.4 %all-to-all-start.4 = ((bf16[8,8,512]{2,1,0:T(8,128)(2,1)}), bf16[8,8,512]{2,1,0:T(8,128)(2,1)S(1)}, u32[]{:S(2)}, u32[]{:S(2)}) async-start(bf16[8,8,512]{2,1,0:T(8,128)(2,1)} %broadcast_in_dim.13), calls=%async_computation.4 | async-start | bytes 131072 | tf_op jit(solution)/shard_map/all_to_all | solution.py:11
  209.5 9.2 %all-to-all-done.4 = bf16[8,8,512]{2,1,0:T(8,128)(2,1)S(1)} async-done(((bf16[8,8,512]{2,1,0:T(8,128)(2,1)}), bf16[8,8,512]{2,1,0:T(8,128)(2,1)S(1)}, u32[]{:S(2)}, u32[]{:S(2)}) %all-to-all-start.4) | async-done | bytes 65568 | tf_op jit(solution)/shard_map/all_to_all | solution.py:11
  218.7 22.7 %all_to_all.42 = bf16[32,8,256]{2,1,0:T(8,128)(2,1)S(1)} all-to-all(bf16[32,8,256]{2,1,0:T(8,128)(2,1)S(1)} %broadcast_in_dim.14), channel_id=1, replica_groups=mesh['emit'=8,'client'=32] {'client'}, dimensions={0} | all-to-all | bytes 262144 | tf_op jit(solution)/shard_map/all_to_all | solution.py:11
  241.4 51.7 %reduce-scatter.2.cloned.1.call-done = bf16[256,768]{1,0:T(8,128)(2,1)} async-done(((bf16[2048,768]{1,0:T(8,128)(2,1)}), bf16[256,768]{1,0:T(8,128)(2,1)}) %reduce-scatter.2.cloned.1.call-update) | async-done | bytes 393232 | tf_op jit(solution)/shard_map/reduce_scatter | solution.py:93
  293.2 6.8 %all-to-all-start.5 = ((bf16[32,8,768]{2,1,0:T(8,128)(2,1)}), bf16[32,8,768]{2,1,0:T(8,128)(2,1)S(1)}, u32[]{:S(2)}, u32[]{:S(2)}) async-start(bf16[32,8,768]{2,1,0:T(8,128)(2,1)} %bitcast.45), calls=%async_computation.6 | async-start | bytes 786432 | tf_op jit(solution)/shard_map/all_to_all | solution.py:42
  300.0 0.6 copy.15
  300.6 1.1 convolution_bitcast_fusion
  301.7 12.3 %all-to-all-done.5 = bf16[32,8,768]{2,1,0:T(8,128)(2,1)S(1)} async-done(((bf16[32,8,768]{2,1,0:T(8,128)(2,1)}), bf16[32,8,768]{2,1,0:T(8,128)(2,1)S(1)}, u32[]{:S(2)}, u32[]{:S(2)}) %all-to-all-start.5) | async-done | bytes 393248 | tf_op jit(solution)/shard_map/all_to_all | solution.py:42
  314.0 0.7 convert_reduce_fusion
  (10 shorter events, 0.1 us)
Async XLA Ops:
  7.2 1.2 copy-start
  7.2 40.4 %copy-start.4 = (bf16[256,768]{1,0:T(8,128)(2,1)S(1)}, bf16[256,768]{1,0:T(8,128)(2,1)}, u32[]{:S(2)}) copy-start(bf16[256,768]{1,0:T(8,128)(2,1)} %param.13) | copy-start | bytes 1179652
  49.5 9.4 %copy-start.6 = (s32[256]{0:T(256)S(1)}, s32[256]{0:T(256)}, u32[]{:S(2)}) copy-start(s32[256]{0:T(256)} %param.9) | copy-start | bytes 3076
  49.5 81.6 %all-to-all-start.1 = ((bf16[8,256,768]{2,1,0:T(8,128)(2,1)}), bf16[8,256,768]{2,1,0:T(8,128)(2,1)}, u32[]{:S(2)}, u32[]{:S(2)}) async-start(bf16[8,256,768]{2,1,0:T(8,128)(2,1)} %stack.2), calls=%async_computation.1 | async-start | bytes 6291456 | tf_op jit(solution)/shard_map/all_to_all | solution.py:71
  58.9 4.1 %copy-start.1 = (f32[125,2048]{1,0:T(8,128)}, f32[125,2048]{1,0:T(8,128)S(1)}, u32[]{:S(2)}) copy-start(f32[125,2048]{1,0:T(8,128)S(1)} %convert_element_type.76) | copy-start | bytes 3072004
  139.3 10.4 %copy-start.5 = (s32[4096]{0:T(1024)S(1)}, s32[4096]{0:T(1024)}, u32[]{:S(2)}) copy-start(s32[4096]{0:T(1024)} %param.8) | copy-start | bytes 49156
  145.3 13.8 %all-to-all-start.2 = ((f32[8,8,512]{2,1,0:T(8,128)}), f32[8,8,512]{2,1,0:T(8,128)S(1)}, u32[]{:S(2)}, u32[]{:S(2)}) async-start(f32[8,8,512]{2,1,0:T(8,128)} %broadcast_in_dim.11), calls=%async_computation.2 | async-start | bytes 262144 | tf_op jit(solution)/shard_map/all_to_all | solution.py:11
  149.6 143.5 %reduce-scatter.2.cloned.1.call-start = ((), (), s32[]{:S(2)}) async-start(), calls=%async_computation.9 | async-start | bytes 3538944 | tf_op jit(solution)/shard_map/reduce_scatter | solution.py:93
  171.3 5.3 %copy-start.2 = (f32[125,2048]{1,0:T(8,128)S(1)}, f32[125,2048]{1,0:T(8,128)}, u32[]{:S(2)}) copy-start(f32[125,2048]{1,0:T(8,128)} %copy-done.1) | copy-start | bytes 3072004
  175.4 1.1 copy-start.7
  182.3 1.2 copy-start.3
  191.6 13.8 %all-to-all-start.6 = ((bf16[8,8,256]{2,1,0:T(8,128)(2,1)}), bf16[8,8,256]{2,1,0:T(8,128)(2,1)S(1)}, u32[]{:S(2)}, u32[]{:S(2)}) async-start(bf16[8,8,256]{2,1,0:T(8,128)(2,1)} %bitcast.9), calls=%async_computation.7 | async-start | bytes 65536 | tf_op jit(solution)/shard_map/all_to_all | solution.py:42
  206.1 12.6 %all-to-all-start.4 = ((bf16[8,8,512]{2,1,0:T(8,128)(2,1)}), bf16[8,8,512]{2,1,0:T(8,128)(2,1)S(1)}, u32[]{:S(2)}, u32[]{:S(2)}) async-start(bf16[8,8,512]{2,1,0:T(8,128)(2,1)} %broadcast_in_dim.13), calls=%async_computation.4 | async-start | bytes 131072 | tf_op jit(solution)/shard_map/all_to_all | solution.py:11
  293.2 20.9 %all-to-all-start.5 = ((bf16[32,8,768]{2,1,0:T(8,128)(2,1)}), bf16[32,8,768]{2,1,0:T(8,128)(2,1)S(1)}, u32[]{:S(2)}, u32[]{:S(2)}) async-start(bf16[32,8,768]{2,1,0:T(8,128)(2,1)} %bitcast.45), calls=%async_computation.6 | async-start | bytes 786432 | tf_op jit(solution)/shard_map/all_to_all | solution.py:42
Sparse Core Ops, SparseCore 0:
  182.4 110.7 reduce-scatter.1
